TPU v7x, 256 devices: a whole 4x4x8 slice. The times are simulated.
256 devices in a mesh: dp: 8 (over y, z_hi), tile: 32 (over x, z_lo, core).
Axes of the slice: x: 4, y: 4, z: 8 (z_hi: 2, z_lo: 4; z = z_hi * 4 + z_lo), core: 2. Of those that a mesh axis runs over, the one named last changes fastest.
Arguments:
- videos: bfloat16 [8, 32, 32, 64, 512], P('dp', 'tile'), may hold values from -6 to 6
- spatial_filter: bfloat16 [9, 512, 512], P(None, 'dp'), may hold values from -0.09375 to 0.09375
- temporal_filter: bfloat16 [3, 512, 512], P(None, 'dp'), may hold values from -0.15625 to 0.15625
- spatial_bias: float32 [512], replicated, may hold values from -3 to 3
- temporal_bias: float32 [512], replicated, may hold values from -3 to 3
Outputs:
- output: bfloat16 [8, 32, 32, 64, 512], P('dp', 'tile')
All inputs are finite; a program needn't handle non-finite values.
Results may differ from a plain program's by a relative error of at most 0.0044.
Values may be sent and summed in bfloat16 or wider, within the bound.
A program may use at most 128 MiB of HBM per device.

v0:
```python
import jax
import jax.numpy as jnp
from jax import lax
from jax.sharding import PartitionSpec as P


def padded_2(block, sides, width):
    for axis, dim in sides:
        count = lax.axis_size(axis)
        forward = [(i, i + 1) for i in range(count - 1)]
        backward = [(target, source) for source, target in forward]
        low = lax.ppermute(
            lax.slice_in_dim(block, block.shape[dim] - width, None, axis=dim), axis, forward
        )
        high = lax.ppermute(lax.slice_in_dim(block, 0, width, axis=dim), axis, backward)
        block = jnp.concatenate([low, block, high], axis=dim)
    return block


def spatial_term(padded, weight_piece):
    width = weight_piece.shape[1]
    height = padded.shape[2] - 2
    breadth = padded.shape[3] - 2
    columns = jnp.concatenate(
        [
            padded[:, :, row_off : row_off + height, col_off : col_off + breadth, :]
            for row_off in range(3)
            for col_off in range(3)
        ],
        axis=4,
    )
    matrix = weight_piece.reshape(9 * width, weight_piece.shape[2])
    return jnp.dot(columns.reshape(-1, 9 * width), matrix, preferred_element_type=jnp.float32)


def temporal_term(framed, weight_piece):
    width = weight_piece.shape[1]
    frames = framed.shape[1] - 2
    columns = jnp.concatenate([framed[:, lag : lag + frames] for lag in range(3)], axis=4)
    matrix = weight_piece.reshape(3 * width, weight_piece.shape[2])
    return jnp.dot(columns.reshape(-1, 3 * width), matrix, preferred_element_type=jnp.float32)


def per_device(videos, spatial_filter, temporal_filter, spatial_bias, temporal_bias):
    samples, frames, height, breadth, channels = videos.shape
    count_frames = videos.shape[1]
    padded = jnp.pad(videos, ((0, 0), (0, 0), (1, 1), (1, 1), (0, 0)))
    summed = spatial_term(padded, lax.all_gather(spatial_filter, "dp", axis=1, tiled=True))
    activated = jax.nn.silu(summed + spatial_bias).astype(jnp.bfloat16)
    hidden = activated.reshape(samples, count_frames, height, breadth, channels)
    framed = padded_2(hidden, (("tile", 1),), 1)
    result = temporal_term(framed, lax.all_gather(temporal_filter, "dp", axis=1, tiled=True))
    return (result + temporal_bias).astype(jnp.bfloat16).reshape(videos.shape)


def solution(mesh):
    return jax.shard_map(
        per_device,
        mesh=mesh,
        in_specs=(
            P("dp", "tile", None, None, None),
            P(None, "dp", None),
            P(None, "dp", None),
            P(),
            P(),
        ),
        out_specs=P("dp", "tile", None, None, None),
        check_vma=False,
    )
```

profile of v0, /device:TPU:1, one launch (start us, length us, event | category | flops | bytes accessed | tf_op | source)
XLA Modules:
  0.0 228.2 jit_solution(13520640981759495450)
XLA Ops:
  6.5 0.0 copy-start
  6.5 0.0 all-gather.3.cloned.1.call-start
  6.5 0.7 all-gather.3.cloned.1.call-update
  7.3 0.0 all-gather.5.cloned.1.call-start
  7.3 0.7 all-gather.5.cloned.1.call-update
  8.0 3.5 %slice_dynamic-update-slice_fusion.7 = bf16[1,1,32,64,4608]{4,3,2,1,0:T(8,128)(2,1)} fusion(bf16[1,1,32,64,512]{4,3,2,1,0:T(8,128)(2,1)} %param.5), kind=kLoop, calls=%fused_computation.15 | loop fusion | bytes 4194304
  11.5 0.0 copy-done
  11.5 1.6 slice_dynamic-update-slice_fusion.6
  13.1 2.5 %slice_dynamic-update-slice_fusion.5 = bf16[1,1,32,64,4608]{4,3,2,1,0:T(8,128)(2,1)} fusion(bf16[1,1,32,64,4608]{4,3,2,1,0:T(8,128)(2,1)} %slice_dynamic-update-slice_fusion.6, bf16[1,1,32,64,512]{4,3,2,1,0:T(8,128)(2,1)S(1)} %copy-done), kind=kLoop, calls=%fused_computation.13 | loop fusion | bytes 4194304
  15.7 2.7 %slice_dynamic-update-slice_fusion.4 = bf16[1,1,32,64,4608]{4,3,2,1,0:T(8,128)(2,1)} fusion(bf16[1,1,32,64,4608]{4,3,2,1,0:T(8,128)(2,1)} %slice_dynamic-update-slice_fusion.5, bf16[1,1,32,64,512]{4,3,2,1,0:T(8,128)(2,1)S(1)} %copy-done), kind=kLoop, calls=%fused_computation.12 | loop fusion | bytes 4194304
  18.4 1.6 constant_dynamic-update-slice_fusion
  20.0 2.5 %slice_dynamic-update-slice_fusion.3 = bf16[1,1,32,64,4608]{4,3,2,1,0:T(8,128)(2,1)} fusion(bf16[1,1,32,64,4608]{4,3,2,1,0:T(8,128)(2,1)} %constant_dynamic-update-slice_fusion, bf16[1,1,32,64,512]{4,3,2,1,0:T(8,128)(2,1)S(1)} %copy-done), kind=kLoop, calls=%fused_computation.11 | loop fusion | bytes 4194304
  22.5 2.7 %slice_dynamic-update-slice_fusion.2 = bf16[1,1,32,64,4608]{4,3,2,1,0:T(8,128)(2,1)} fusion(bf16[1,1,32,64,4608]{4,3,2,1,0:T(8,128)(2,1)} %slice_dynamic-update-slice_fusion.3, bf16[1,1,32,64,512]{4,3,2,1,0:T(8,128)(2,1)S(1)} %copy-done), kind=kLoop, calls=%fused_computation.10 | loop fusion | bytes 4194304
  25.2 0.0 copy-start.1
  25.2 1.6 slice_dynamic-update-slice_fusion.1
  26.9 2.6 %slice_dynamic-update-slice_fusion = bf16[1,1,32,64,4608]{4,3,2,1,0:T(8,128)(2,1)} fusion(bf16[1,1,32,64,4608]{4,3,2,1,0:T(8,128)(2,1)} %slice_dynamic-update-slice_fusion.1, bf16[1,1,32,64,512]{4,3,2,1,0:T(8,128)(2,1)S(1)} %copy-done), kind=kLoop, calls=%fused_computation.8 | loop fusion | bytes 4194304 | tf_op jit(solution)/shard_map/concatenate | solution.py:24
  29.4 98.5 %all-gather.3.cloned.1.call-done = bf16[9,512,512]{2,1,0:T(8,128)(2,1)} async-done(((bf16[9,64,512]{2,1,0:T(8,128)(2,1)}), bf16[9,512,512]{2,1,0:T(8,128)(2,1)}) %all-gather.3.cloned.1.call-update) | async-done | bytes 4718608 | tf_op jit(solution)/shard_map/all_gather | solution.py:48
  127.9 0.0 copy-done.1
  127.9 0.0 copy-start.2
  127.9 15.8 %multiply_convert_fusion = bf16[2048,512]{1,0:T(8,128)(2,1)S(1)} fusion(bf16[2048,4608]{1,0:T(8,128)(2,1)} %bitcast, bf16[4608,512]{1,0:T(8,128)(2,1)} %bitcast.10, f32[512]{0:T(512)S(1)} %copy-done.1), kind=kOutput, calls=%fused_computation.7 | convolution fusion | flops 9669967872 | bytes 25692160 | tf_op jit(solution)/shard_map/dot_general | solution.py:33
  143.7 3.4 %collective-permute-start = (bf16[1,1,32,64,512]{4,3,2,1,0:T(8,128)(2,1)S(1)}, bf16[1,1,32,64,512]{4,3,2,1,0:T(8,128)(2,1)}, u32[]{:S(2)}, u32[]{:S(2)}) collective-permute-start(bf16[1,1,32,64,512]{4,3,2,1,0:T(8,128)(2,1)S(1)} %bitcast.11), channel_id=1, source_target_pairs={{0,1},{1,2},{2,3},{3,4},{4,5},{5,6},{6,7},{7,8},{8,9},{9,10},{10,1... | collective-permute-start | bytes 6291464 | tf_op jit(solution)/shard_map/ppermute | solution.py:12
  147.2 2.7 %collective-permute-start.1 = (bf16[1,1,32,64,512]{4,3,2,1,0:T(8,128)(2,1)S(1)}, bf16[1,1,32,64,512]{4,3,2,1,0:T(8,128)(2,1)}, u32[]{:S(2)}, u32[]{:S(2)}) collective-permute-start(bf16[1,1,32,64,512]{4,3,2,1,0:T(8,128)(2,1)S(1)} %bitcast.12), channel_id=1, source_target_pairs={{1,0},{2,1},{3,2},{4,3},{5,4},{6,5},{7,6},{8,7},{9,8},{10,9},{11,1... | collective-permute-start | bytes 6291464 | tf_op jit(solution)/shard_map/ppermute | solution.py:15
  149.8 46.0 %all-gather.5.cloned.1.call-done = bf16[3,512,512]{2,1,0:T(8,128)(2,1)} async-done(((bf16[3,64,512]{2,1,0:T(8,128)(2,1)}), bf16[3,512,512]{2,1,0:T(8,128)(2,1)}) %all-gather.5.cloned.1.call-update) | async-done | bytes 1572880 | tf_op jit(solution)/shard_map/all_gather | solution.py:52
  195.8 0.0 collective-permute-done
  195.8 18.1 %collective-permute-done.1 = bf16[1,1,32,64,512]{4,3,2,1,0:T(8,128)(2,1)} collective-permute-done((bf16[1,1,32,64,512]{4,3,2,1,0:T(8,128)(2,1)S(1)}, bf16[1,1,32,64,512]{4,3,2,1,0:T(8,128)(2,1)}, u32[]{:S(2)}, u32[]{:S(2)}) %collective-permute-start.1) | collective-permute-done | bytes 2097184 | tf_op jit(solution)/shard_map/ppermute | solution.py:15
  213.9 0.0 copy-done.2
  214.0 7.4 %add_convert_fusion = bf16[2048,512]{1,0:T(8,128)(2,1)} fusion(bf16[1536,512]{1,0:T(8,128)(2,1)} %bitcast.13, bf16[2048,512]{1,0:T(8,128)(2,1)} %bitcast.4, bf16[2048,512]{1,0:T(8,128)(2,1)S(1)} %multiply_convert_fusion, bf16[2048,512]{1,0:T(8,128)(2,1)} %bitcast.3, f32[512]{0:T(512)S(1)} %copy-done.2), kind=kOutput, calls=%fused_computation.6 | convolution fusion | flops 3242196992 | bytes 9963520 | tf_op jit(solution)/shard_map/dot_general | solution.py:41
Async XLA Ops:
  6.5 5.0 %copy-start = (bf16[1,1,32,64,512]{4,3,2,1,0:T(8,128)(2,1)S(1)}, bf16[1,1,32,64,512]{4,3,2,1,0:T(8,128)(2,1)}, u32[]{:S(2)}) copy-start(bf16[1,1,32,64,512]{4,3,2,1,0:T(8,128)(2,1)} %param.5) | copy-start | bytes 6291460
  6.5 121.4 %all-gather.3.cloned.1.call-start = ((), (), s32[]{:S(2)}) async-start(), calls=%async_computation | async-start | bytes 5308416 | tf_op jit(solution)/shard_map/all_gather | solution.py:48
  7.3 188.5 %all-gather.5.cloned.1.call-start = ((), (), s32[]{:S(2)}) async-start(), calls=%async_computation.1 | async-start | bytes 1769472 | tf_op jit(solution)/shard_map/all_gather | solution.py:52
  25.2 102.7 %copy-start.1 = (f32[512]{0:T(512)S(1)}, f32[512]{0:T(512)}, u32[]{:S(2)}) copy-start(f32[512]{0:T(512)} %param.8) | copy-start | bytes 6148
  127.9 86.0 %copy-start.2 = (f32[512]{0:T(512)S(1)}, f32[512]{0:T(512)}, u32[]{:S(2)}) copy-start(f32[512]{0:T(512)} %param.9) | copy-start | bytes 6148
  143.7 52.1 %collective-permute-start = (bf16[1,1,32,64,512]{4,3,2,1,0:T(8,128)(2,1)S(1)}, bf16[1,1,32,64,512]{4,3,2,1,0:T(8,128)(2,1)}, u32[]{:S(2)}, u32[]{:S(2)}) collective-permute-start(bf16[1,1,32,64,512]{4,3,2,1,0:T(8,128)(2,1)S(1)} %bitcast.11), channel_id=1, source_target_pairs={{0,1},{1,2},{2,3},{3,4},{4,5},{5,6},{6,7},{7,8},{8,9},{9,10},{10,1... | collective-permute-start | bytes 6291464 | tf_op jit(solution)/shard_map/ppermute | solution.py:12
  147.2 66.8 %collective-permute-start.1 = (bf16[1,1,32,64,512]{4,3,2,1,0:T(8,128)(2,1)S(1)}, bf16[1,1,32,64,512]{4,3,2,1,0:T(8,128)(2,1)}, u32[]{:S(2)}, u32[]{:S(2)}) collective-permute-start(bf16[1,1,32,64,512]{4,3,2,1,0:T(8,128)(2,1)S(1)} %bitcast.12), channel_id=1, source_target_pairs={{1,0},{2,1},{3,2},{4,3},{5,4},{6,5},{7,6},{8,7},{9,8},{10,9},{11,1... | collective-permute-start | bytes 6291464 | tf_op jit(solution)/shard_map/ppermute | solution.py:15
Sparse Core Ops, SparseCore 0:
  10.0 117.9 all-gather.2
  130.6 65.1 all-gather.4
where the time goes:
time: 228 us
  waiting for transfers between devices  164 us (72%)
  matrix products  23.2 us (10%)
  local copies, waits for them, and re-layouts  21.4 us (9%)
  between operations  13.4 us (6%)
  starting transfers between devices  6.15 us (3%)
    all_gather x1, waiting for transfers between devices, per_device(): lax.all_gather(spatial_filter, 'dp', axis=1, tiled=True)  98.5 us
    all_gather x1, waiting for transfers between devices, per_device(): lax.all_gather(temporal_filter, 'dp', axis=1, tiled=True)  46 us
    unnamed x14, local copies, waits for them, and re-layouts  18.9 us
    ppermute x1, waiting for transfers between devices, padded_2(): lax.ppermute(lax.slice_in_dim(block, 0, width, axis=dim), axis, backward)  18.1 us
    dot_general x1, matrix products, spatial_term(): jnp.dot(columns.reshape(-1, 9 * width), matrix, preferred_element_type=jn...  15.8 us
    dot_general x1, matrix products, temporal_term(): jnp.dot(columns.reshape(-1, 3 * width), matrix, preferred_element_type=jn...  7.42 us
  transfers between devices with their start and end apart: 4, of which 3 were waited for; matrix products, arithmetic and copies ran while one was open for 16% of the time, Pallas kernels for 0%

commit v1 on v0

--- a/solution.py
+++ b/solution.py
@@ -2,6 +2,11 @@
 import jax.numpy as jnp
 from jax import lax
 from jax.sharding import PartitionSpec as P
+
+
+def gather_over(block, axis, dim):
+    sent = jnp.stack([block] * lax.axis_size(axis))
+    return jnp.concatenate(lax.all_to_all(sent, axis, 0, 0), axis=dim)
 
 
 def padded_2(block, sides, width):
@@ -45,7 +50,7 @@
     samples, frames, height, breadth, channels = videos.shape
     count_frames = videos.shape[1]
     padded = jnp.pad(videos, ((0, 0), (0, 0), (1, 1), (1, 1), (0, 0)))
-    summed = spatial_term(padded, lax.all_gather(spatial_filter, "dp", axis=1, tiled=True))
+    summed = spatial_term(padded, gather_over(spatial_filter, "dp", 1))
     activated = jax.nn.silu(summed + spatial_bias).astype(jnp.bfloat16)
     hidden = activated.reshape(samples, count_frames, height, breadth, channels)
     framed = padded_2(hidden, (("tile", 1),), 1)

time: 228 us -> 236 us (1.035)
  the two profiles are of different devices: /device:TPU:1 before, /device:TPU:29 now
where the time goes in v1:
time: 236 us; the launch traced here: 235 us
  waiting for transfers between devices  94.3 us (40%)
  starting transfers between devices  79.5 us (34%)
  local copies, waits for them, and re-layouts  26.4 us (11%)
  matrix products  21.8 us (9%)
  between operations  13.5 us (6%)
    all_to_all x1, waiting for transfers between devices, gather_over(): return jnp.concatenate(lax.all_to_all(sent, axis, 0, 0), axis=dim)  68.2 us
    ppermute x1, starting transfers between devices, padded_2(): lax.ppermute(lax.slice_in_dim(block, block.shape[dim] - width, None, axis...  66.5 us
    ppermute x1, waiting for transfers between devices, padded_2(): lax.ppermute(lax.slice_in_dim(block, block.shape[dim] - width, None, axis...  20.8 us
    unnamed x14, local copies, waits for them, and re-layouts  17.2 us
    dot_general x1, matrix products, spatial_term(): jnp.dot(columns.reshape(-1, 9 * width), matrix, preferred_element_type=jn...  14.3 us
    all_to_all x1, starting transfers between devices, gather_over(): return jnp.concatenate(lax.all_to_all(sent, axis, 0, 0), axis=dim)  10.9 us
    dot_general x1, matrix products, temporal_term(): jnp.dot(columns.reshape(-1, 3 * width), matrix, preferred_element_type=jn...  7.43 us
  transfers between devices with their start and end apart: 4, of which 3 were waited for; matrix products, arithmetic and copies ran while one was open for 16% of the time, Pallas kernels for 0%

profile of v1, /device:TPU:29, one launch (start us, length us, event | category | flops | bytes accessed | tf_op | source)
XLA Modules:
  0.0 235.3 jit_solution(7155810471273776231)
XLA Ops:
  6.5 3.9 %stack.2 = bf16[8,9,64,512]{3,2,1,0:T(8,128)(2,1)} broadcast(bf16[9,64,512]{2,1,0:T(8,128)(2,1)} %param.6), dimensions={1,2,3} | broadcast | bytes 5308416 | tf_op jit(solution)/shard_map/stack | solution.py:8
  10.4 0.0 copy-start
  10.4 10.9 %all-to-all-start = ((bf16[8,9,64,512]{3,2,1,0:T(8,128)(2,1)}), bf16[8,9,64,512]{3,2,1,0:T(8,128)(2,1)}, u32[]{:S(2)}, u32[]{:S(2)}) async-start(bf16[8,9,64,512]{3,2,1,0:T(8,128)(2,1)} %stack.2), calls=%async_computation | async-start | bytes 9437184 | tf_op jit(solution)/shard_map/all_to_all | solution.py:9
  21.3 0.0 all-gather.2.cloned.1.call-start
  21.3 0.7 all-gather.2.cloned.1.call-update
  22.0 0.0 copy-done
  22.0 2.0 slice_dynamic-update-slice_fusion.7
  24.0 1.6 slice_dynamic-update-slice_fusion.6
  25.7 2.5 %slice_dynamic-update-slice_fusion.5 = bf16[1,1,32,64,4608]{4,3,2,1,0:T(8,128)(2,1)} fusion(bf16[1,1,32,64,4608]{4,3,2,1,0:T(8,128)(2,1)} %slice_dynamic-update-slice_fusion.6, bf16[1,1,32,64,512]{4,3,2,1,0:T(8,128)(2,1)S(1)} %copy-done), kind=kLoop, calls=%fused_computation.13 | loop fusion | bytes 4194304
  28.2 2.7 %slice_dynamic-update-slice_fusion.4 = bf16[1,1,32,64,4608]{4,3,2,1,0:T(8,128)(2,1)} fusion(bf16[1,1,32,64,4608]{4,3,2,1,0:T(8,128)(2,1)} %slice_dynamic-update-slice_fusion.5, bf16[1,1,32,64,512]{4,3,2,1,0:T(8,128)(2,1)S(1)} %copy-done), kind=kLoop, calls=%fused_computation.12 | loop fusion | bytes 4194304
  30.9 1.5 constant_dynamic-update-slice_fusion
  32.4 2.6 %slice_dynamic-update-slice_fusion.3 = bf16[1,1,32,64,4608]{4,3,2,1,0:T(8,128)(2,1)} fusion(bf16[1,1,32,64,4608]{4,3,2,1,0:T(8,128)(2,1)} %constant_dynamic-update-slice_fusion, bf16[1,1,32,64,512]{4,3,2,1,0:T(8,128)(2,1)S(1)} %copy-done), kind=kLoop, calls=%fused_computation.11 | loop fusion | bytes 4194304
  35.0 2.7 %slice_dynamic-update-slice_fusion.2 = bf16[1,1,32,64,4608]{4,3,2,1,0:T(8,128)(2,1)} fusion(bf16[1,1,32,64,4608]{4,3,2,1,0:T(8,128)(2,1)} %slice_dynamic-update-slice_fusion.3, bf16[1,1,32,64,512]{4,3,2,1,0:T(8,128)(2,1)S(1)} %copy-done), kind=kLoop, calls=%fused_computation.10 | loop fusion | bytes 4194304
  37.7 1.6 slice_dynamic-update-slice_fusion.1
  39.3 2.6 %slice_dynamic-update-slice_fusion = bf16[1,1,32,64,4608]{4,3,2,1,0:T(8,128)(2,1)} fusion(bf16[1,1,32,64,4608]{4,3,2,1,0:T(8,128)(2,1)} %slice_dynamic-update-slice_fusion.1, bf16[1,1,32,64,512]{4,3,2,1,0:T(8,128)(2,1)S(1)} %copy-done), kind=kLoop, calls=%fused_computation.8 | loop fusion | bytes 4194304 | tf_op jit(solution)/shard_map/concatenate | solution.py:29
  41.8 0.0 copy-start.1
  41.8 68.2 %all-to-all-done = bf16[8,9,64,512]{3,2,1,0:T(8,128)(2,1)} async-done(((bf16[8,9,64,512]{3,2,1,0:T(8,128)(2,1)}), bf16[8,9,64,512]{3,2,1,0:T(8,128)(2,1)}, u32[]{:S(2)}, u32[]{:S(2)}) %all-to-all-start) | async-done | bytes 4718624 | tf_op jit(solution)/shard_map/all_to_all | solution.py:9
  110.1 2.7 %copy.6 = bf16[8,9,64,512]{3,2,0,1:T(8,128)(2,1)S(1)} copy(bf16[8,9,64,512]{3,2,1,0:T(8,128)(2,1)} %all-to-all-done) | data formatting | bytes 9437184 | tf_op jit(solution)/shard_map/all_to_all | solution.py:9
  112.8 0.0 copy-done.1
  112.8 0.0 copy-start.2
  112.8 14.3 %multiply_convert_fusion = bf16[2048,512]{1,0:T(8,128)(2,1)S(1)} fusion(bf16[2048,4608]{1,0:T(8,128)(2,1)} %bitcast, bf16[4608,512]{1,0:T(8,128)(2,1)S(1)} %bitcast.12, f32[512]{0:T(512)S(1)} %copy-done.1), kind=kOutput, calls=%fused_computation.7 | convolution fusion | flops 9669967872 | bytes 25692160 | tf_op jit(solution)/shard_map/dot_general | solution.py:38
  127.1 66.5 %collective-permute-start = (bf16[1,1,32,64,512]{4,3,2,1,0:T(8,128)(2,1)S(1)}, bf16[1,1,32,64,512]{4,3,2,1,0:T(8,128)(2,1)}, u32[]{:S(2)}, u32[]{:S(2)}) collective-permute-start(bf16[1,1,32,64,512]{4,3,2,1,0:T(8,128)(2,1)S(1)} %bitcast.13), channel_id=1, source_target_pairs={{0,1},{1,2},{2,3},{3,4},{4,5},{5,6},{6,7},{7,8},{8,9},{9,10},{10,1... | collective-permute-start | bytes 6291464 | tf_op jit(solution)/shard_map/ppermute | solution.py:17
  193.6 2.1 collective-permute-start.1
  195.7 0.0 all-gather.2.cloned.1.call-done
  195.7 20.8 %collective-permute-done = bf16[1,1,32,64,512]{4,3,2,1,0:T(8,128)(2,1)} collective-permute-done((bf16[1,1,32,64,512]{4,3,2,1,0:T(8,128)(2,1)S(1)}, bf16[1,1,32,64,512]{4,3,2,1,0:T(8,128)(2,1)}, u32[]{:S(2)}, u32[]{:S(2)}) %collective-permute-start) | collective-permute-done | bytes 2097184 | tf_op jit(solution)/shard_map/ppermute | solution.py:17
  216.6 4.5 %collective-permute-done.1 = bf16[1,1,32,64,512]{4,3,2,1,0:T(8,128)(2,1)} collective-permute-done((bf16[1,1,32,64,512]{4,3,2,1,0:T(8,128)(2,1)S(1)}, bf16[1,1,32,64,512]{4,3,2,1,0:T(8,128)(2,1)}, u32[]{:S(2)}, u32[]{:S(2)}) %collective-permute-start.1) | collective-permute-done | bytes 2097184 | tf_op jit(solution)/shard_map/ppermute | solution.py:20
  221.1 0.0 copy-done.2
  221.1 7.4 %add_convert_fusion = bf16[2048,512]{1,0:T(8,128)(2,1)} fusion(bf16[1536,512]{1,0:T(8,128)(2,1)} %bitcast.15, bf16[2048,512]{1,0:T(8,128)(2,1)} %bitcast.5, bf16[2048,512]{1,0:T(8,128)(2,1)S(1)} %multiply_convert_fusion, bf16[2048,512]{1,0:T(8,128)(2,1)} %bitcast.4, f32[512]{0:T(512)S(1)} %copy-done.2), kind=kOutput, calls=%fused_computation.6 | convolution fusion | flops 3242196992 | bytes 9963520 | tf_op jit(solution)/shard_map/dot_general | solution.py:46
Async XLA Ops:
  10.4 11.6 %copy-start = (bf16[1,1,32,64,512]{4,3,2,1,0:T(8,128)(2,1)S(1)}, bf16[1,1,32,64,512]{4,3,2,1,0:T(8,128)(2,1)}, u32[]{:S(2)}) copy-start(bf16[1,1,32,64,512]{4,3,2,1,0:T(8,128)(2,1)} %param.5) | copy-start | bytes 6291460
  10.4 99.7 %all-to-all-start = ((bf16[8,9,64,512]{3,2,1,0:T(8,128)(2,1)}), bf16[8,9,64,512]{3,2,1,0:T(8,128)(2,1)}, u32[]{:S(2)}, u32[]{:S(2)}) async-start(bf16[8,9,64,512]{3,2,1,0:T(8,128)(2,1)} %stack.2), calls=%async_computation | async-start | bytes 9437184 | tf_op jit(solution)/shard_map/all_to_all | solution.py:9
  21.3 174.4 %all-gather.2.cloned.1.call-start = ((), (), s32[]{:S(2)}) async-start(), calls=%async_computation.1 | async-start | bytes 1769472 | tf_op jit(solution)/shard_map/all_gather | solution.py:57
  41.8 71.0 %copy-start.1 = (f32[512]{0:T(512)S(1)}, f32[512]{0:T(512)}, u32[]{:S(2)}) copy-start(f32[512]{0:T(512)} %param.8) | copy-start | bytes 6148
  112.8 108.3 %copy-start.2 = (f32[512]{0:T(512)S(1)}, f32[512]{0:T(512)}, u32[]{:S(2)}) copy-start(f32[512]{0:T(512)} %param.9) | copy-start | bytes 6148
  127.1 89.4 %collective-permute-start = (bf16[1,1,32,64,512]{4,3,2,1,0:T(8,128)(2,1)S(1)}, bf16[1,1,32,64,512]{4,3,2,1,0:T(8,128)(2,1)}, u32[]{:S(2)}, u32[]{:S(2)}) collective-permute-start(bf16[1,1,32,64,512]{4,3,2,1,0:T(8,128)(2,1)S(1)} %bitcast.13), channel_id=1, source_target_pairs={{0,1},{1,2},{2,3},{3,4},{4,5},{5,6},{6,7},{7,8},{8,9},{9,10},{10,1... | collective-permute-start | bytes 6291464 | tf_op jit(solution)/shard_map/ppermute | solution.py:17
  193.6 27.5 %collective-permute-start.1 = (bf16[1,1,32,64,512]{4,3,2,1,0:T(8,128)(2,1)S(1)}, bf16[1,1,32,64,512]{4,3,2,1,0:T(8,128)(2,1)}, u32[]{:S(2)}, u32[]{:S(2)}) collective-permute-start(bf16[1,1,32,64,512]{4,3,2,1,0:T(8,128)(2,1)S(1)} %bitcast.14), channel_id=1, source_target_pairs={{1,0},{2,1},{3,2},{4,3},{5,4},{6,5},{7,6},{8,7},{9,8},{10,9},{11,1... | collective-permute-start | bytes 6291464 | tf_op jit(solution)/shard_map/ppermute | solution.py:20
Sparse Core Ops, SparseCore 0:
  24.7 129.6 all-gather.1
